TPU v7x, 32 devices: a whole 2x2x4 slice. The times are simulated.
32 devices in a mesh: seq: 16 (over z, y, x), head: 2 (over core).
Axes of the slice: x: 2, y: 2, z: 4, core: 2. Of those that a mesh axis runs over, the one named last changes fastest.
Arguments:
- queries: bfloat16 [6144, 3072], P('seq', 'head'), may hold values from -6 to 6
- keys: bfloat16 [6144, 3072], P('seq', 'head'), may hold values from -6 to 6
- values: bfloat16 [6144, 3072], P('seq', 'head'), may hold values from -6 to 6
- text_keys: bfloat16 [512, 3072], P('seq', 'head'), may hold values from -6 to 6
- text_values: bfloat16 [512, 3072], P('seq', 'head'), may hold values from -6 to 6
- neighbours: int32 [16, 5], P('seq'), may hold values from -1 to 15, as said below
- clip_lengths: int32 [4], replicated, may hold values from 1 to 7, as said below
- text_lengths: int32 [4], replicated, may hold values from 1 to 224, as said below
- out_weight: bfloat16 [3072, 3072], P('head'), may hold values from -0.109375 to 0.109375
Outputs:
- mixed: bfloat16 [6144, 3072], P(('seq', 'head'))
Inputs may be any that keep to these rules, and one draw needn't show every extreme that they name: Clips lie end to end and fill all 16 tiles; each clip is laid out in frames of 1 to 3 tiles, and a tile lists itself, its neighbours within its frame and the tiles at the same place in the frames before and after, all inside its clip. `clip_lengths`: the lengths sum to 16. `text_lengths`: A clip's text length is at most its tiles times 32; every clip of 7 tiles fills all its text slots, and every clip of one tile has one text token.
All inputs are finite; a program needn't handle non-finite values.
Results may differ from a plain program's by a relative error of at most 0.012.
Values may be sent and summed in bfloat16 or wider, within the bound.
A program may use at most 192 MiB of HBM per device.

v0:
```python
import jax
import jax.numpy as jnp
from jax import lax
from jax.sharding import PartitionSpec as P

HD = 128
REACH = 3
MOST = 7


def passed_along(shard, axis, by):
    length = lax.axis_size(axis)
    pairs = [(i, i + by) for i in range(length) if 0 <= i + by < length]
    return lax.ppermute(shard, axis, pairs)


def attend(rows_q, rows_k, rows_v, mask):
    count = rows_q.shape[0]
    heads = rows_q.shape[1] // HD
    q_heads = rows_q.reshape(count, heads, HD)
    k_heads = rows_k.reshape(rows_k.shape[0], heads, HD)
    v_heads = rows_v.reshape(rows_v.shape[0], heads, HD)
    score = jnp.einsum(
        "qhd,khd->hqk", q_heads, k_heads, preferred_element_type=jnp.float32
    ) * HD ** (-0.5)
    score = jnp.where(mask[None, None, :], score, -1e30)
    top = jnp.max(score, axis=-1)
    weight = jnp.where(mask[None, None, :], jnp.exp(score - top[..., None]), 0.0)
    total = jnp.sum(weight, axis=-1)
    acc = jnp.einsum(
        "hqk,khd->hqd", weight.astype(jnp.bfloat16), v_heads, preferred_element_type=jnp.float32
    )
    return (top, total, acc)


def combine(first, second):
    top = jnp.maximum(first[0], second[0])
    scale_one = jnp.exp(first[0] - top)
    scale_two = jnp.exp(second[0] - top)
    total = first[1] * scale_one + second[1] * scale_two
    acc = first[2] * scale_one[..., None] + second[2] * scale_two[..., None]
    return (top, total, acc)


def body(
    queries,
    keys,
    values,
    text_keys,
    text_values,
    neighbours,
    clip_lengths,
    text_lengths,
    out_weight,
):
    tile = lax.axis_index("seq")
    starts = jnp.cumsum(clip_lengths) - clip_lengths
    clip = jnp.sum((starts <= tile).astype(jnp.int32)) - 1
    picked = jnp.arange(clip_lengths.shape[0], dtype=jnp.int32) == clip
    clip_start = jnp.sum(jnp.where(picked, starts, 0))
    clip_text = jnp.sum(jnp.where(picked, text_lengths, 0))
    text_rows = text_keys.shape[0]
    text_low = clip_start * text_rows
    text_high = text_low + clip_text
    listed = neighbours[0]
    rows = queries.shape[0]
    every_row = jnp.ones((rows,), dtype=bool)
    state = attend(queries, keys, values, every_row)
    for offset in range(-REACH, REACH + 1):
        if offset == 0:
            continue
        present = jnp.any((listed == tile + offset) & (listed >= 0))
        far = passed_along((keys, values), "seq", -offset)
        part = attend(queries, far[0], far[1], jnp.broadcast_to(present, (rows,)))
        state = combine(state, part)
    for offset in range(-(MOST - 1), MOST):
        if offset == 0:
            piece = (text_keys, text_values)
        else:
            piece = passed_along((text_keys, text_values), "seq", -offset)
        global_rows = (tile + offset) * text_rows + jnp.arange(text_rows, dtype=jnp.int32)
        mask = (global_rows >= text_low) & (global_rows < text_high)
        state = combine(state, attend(queries, piece[0], piece[1], mask))
    attended = state[2] / state[1][..., None]
    attended = jnp.transpose(attended, (1, 0, 2)).reshape(rows, -1).astype(jnp.bfloat16)
    return lax.psum_scatter(
        jnp.dot(attended, out_weight, preferred_element_type=jnp.float32).astype(jnp.bfloat16),
        "head",
        scatter_dimension=0,
        tiled=True,
    )


def solution(mesh):
    placed = (
        P("seq", "head"),
        P("seq", "head"),
        P("seq", "head"),
        P("seq", "head"),
        P("seq", "head"),
        P("seq", None),
        P(),
        P(),
        P("head", None),
    )
    return jax.shard_map(
        body, mesh=mesh, in_specs=placed, out_specs=P(("seq", "head"), None), check_vma=False
    )
```

profile of v0, /device:TPU:0, one launch (start us, length us, event | category | flops | bytes accessed | tf_op | source)
XLA Modules:
  0.0 500.7 jit_solution(16754937683333013243)
XLA Ops:
  11.9 11.2 %collective-permute-start.12 = (bf16[32,1536]{1,0:T(8,128)(2,1)}, bf16[32,1536]{1,0:T(8,128)(2,1)}, u32[]{:S(2)}, u32[]{:S(2)}) collective-permute-start(bf16[32,1536]{1,0:T(8,128)(2,1)} %param.12), channel_id=1, source_target_pairs={{0,12},{2,14},{4,16},{6,18},{8,20},{10,22},{12,24},{14,26},{16,28}... | collective-permute-start | bytes 294920 | tf_op jit(solution)/shard_map/ppermute | solution.py:14
  33.7 2.4 copy.48
  36.8 2.4 copy.51
  41.7 2.4 multiply_reduce_fusion
  45.9 2.9 fusion.32
  48.8 5.0 %collective-permute-start.14 = (bf16[32,1536]{1,0:T(8,128)(2,1)S(1)}, bf16[32,1536]{1,0:T(8,128)(2,1)S(1)}, u32[]{:S(2)}, u32[]{:S(2)}) collective-permute-start(bf16[32,1536]{1,0:T(8,128)(2,1)S(1)} %copy-done.75), channel_id=1, source_target_pairs={{0,10},{2,12},{4,14},{6,16},{8,18},{10,20},{12,22},{14,24},{16,26}... | collective-permute-start | bytes 294920 | tf_op jit(solution)/shard_map/ppermute | solution.py:14
  56.1 4.1 collective-permute-start.16
  60.5 1.8 collective-permute-done.16
  62.4 4.8 collective-permute-start.18
  67.6 1.8 collective-permute-done.18
  69.4 3.9 collective-permute-start.20
  75.5 5.9 %collective-permute-start.22 = (bf16[32,1536]{1,0:T(8,128)(2,1)S(1)}, bf16[32,1536]{1,0:T(8,128)(2,1)S(1)}, u32[]{:S(2)}, u32[]{:S(2)}) collective-permute-start(bf16[32,1536]{1,0:T(8,128)(2,1)S(1)} %copy-done.75), channel_id=1, source_target_pairs={{0,2},{2,4},{4,6},{6,8},{8,10},{10,12},{12,14},{14,16},{16,18},{18... | collective-permute-start | bytes 294920 | tf_op jit(solution)/shard_map/ppermute | solution.py:14
  81.8 1.8 collective-permute-done.22
  98.0 11.0 %collective-permute-start.17 = (bf16[32,1536]{1,0:T(8,128)(2,1)}, bf16[32,1536]{1,0:T(8,128)(2,1)S(1)}, u32[]{:S(2)}, u32[]{:S(2)}) collective-permute-start(bf16[32,1536]{1,0:T(8,128)(2,1)} %param.13), channel_id=1, source_target_pairs={{0,8},{2,10},{4,12},{6,14},{8,16},{10,18},{12,20},{14,22},{16,24},... | collective-permute-start | bytes 294920 | tf_op jit(solution)/shard_map/ppermute | solution.py:14
  109.4 2.1 collective-permute-done.17
  111.5 6.6 %collective-permute-start.19 = (bf16[32,1536]{1,0:T(8,128)(2,1)}, bf16[32,1536]{1,0:T(8,128)(2,1)S(1)}, u32[]{:S(2)}, u32[]{:S(2)}) collective-permute-start(bf16[32,1536]{1,0:T(8,128)(2,1)} %param.13), channel_id=1, source_target_pairs={{0,6},{2,8},{4,10},{6,12},{8,14},{10,16},{12,18},{14,20},{16,22},{... | collective-permute-start | bytes 294920 | tf_op jit(solution)/shard_map/ppermute | solution.py:14
  118.1 1.9 fusion.163
  120.8 4.8 collective-permute-start.21
  125.6 1.9 fusion.161
  128.3 3.4 collective-permute-start.23
  131.7 2.0 fusion.159
  134.5 7.9 %collective-permute-start.15 = (bf16[32,1536]{1,0:T(8,128)(2,1)}, bf16[32,1536]{1,0:T(8,128)(2,1)S(1)}, u32[]{:S(2)}, u32[]{:S(2)}) collective-permute-start(bf16[32,1536]{1,0:T(8,128)(2,1)} %param.13), channel_id=1, source_target_pairs={{0,10},{2,12},{4,14},{6,16},{8,18},{10,20},{12,22},{14,24},{16,26}... | collective-permute-start | bytes 294920 | tf_op jit(solution)/shard_map/ppermute | solution.py:14
  142.3 1.9 fusion.157
  145.0 5.7 %collective-permute-start.13 = (bf16[32,1536]{1,0:T(8,128)(2,1)}, bf16[32,1536]{1,0:T(8,128)(2,1)S(1)}, u32[]{:S(2)}, u32[]{:S(2)}) collective-permute-start(bf16[32,1536]{1,0:T(8,128)(2,1)} %param.13), channel_id=1, source_target_pairs={{0,12},{2,14},{4,16},{6,18},{8,20},{10,22},{12,24},{14,26},{16,28}... | collective-permute-start | bytes 294920 | tf_op jit(solution)/shard_map/ppermute | solution.py:14
  150.6 2.0 fusion.153
  154.7 2.0 fusion.151
  158.7 2.0 fusion.149
  161.4 5.7 %collective-permute-start = (bf16[384,1536]{0,1:T(8,128)(2,1)}, bf16[384,1536]{0,1:T(8,128)(2,1)}, u32[]{:S(2)}, u32[]{:S(2)}) collective-permute-start(bf16[384,1536]{0,1:T(8,128)(2,1)} %copy.48), channel_id=1, source_target_pairs={{0,6},{2,8},{4,10},{6,12},{8,14},{10,16},{12,18},{14,20},{16,22},{... | collective-permute-start | bytes 3538952 | tf_op jit(solution)/shard_map/ppermute | solution.py:14
  167.1 1.9 fusion.147
  169.8 7.6 %collective-permute-start.1 = (bf16[384,1536]{1,0:T(8,128)(2,1)}, bf16[384,1536]{1,0:T(8,128)(2,1)}, u32[]{:S(2)}, u32[]{:S(2)}) collective-permute-start(bf16[384,1536]{1,0:T(8,128)(2,1)} %param.11), channel_id=1, source_target_pairs={{0,6},{2,8},{4,10},{6,12},{8,14},{10,16},{12,18},{14,20},{16,22},{... | collective-permute-start | bytes 3538952 | tf_op jit(solution)/shard_map/ppermute | solution.py:14
  177.3 1.9 fusion.145
  180.8 3.5 collective-permute-start.2
  184.3 2.0 fusion.165
  187.0 2.3 collective-permute-start.3
  189.3 1.9 fusion.167
  192.0 24.0 %collective-permute-done.1 = bf16[384,1536]{1,0:T(8,128)(2,1)} collective-permute-done((bf16[384,1536]{1,0:T(8,128)(2,1)}, bf16[384,1536]{1,0:T(8,128)(2,1)}, u32[]{:S(2)}, u32[]{:S(2)}) %collective-permute-start.1) | collective-permute-done | bytes 1179680 | tf_op jit(solution)/shard_map/ppermute | solution.py:14
  216.0 2.3 collective-permute-start.4
  218.3 2.4 copy.56
  220.8 9.1 %collective-permute-start.5 = (bf16[384,1536]{1,0:T(8,128)(2,1)}, bf16[384,1536]{1,0:T(8,128)(2,1)}, u32[]{:S(2)}, u32[]{:S(2)}) collective-permute-start(bf16[384,1536]{1,0:T(8,128)(2,1)} %param.11), channel_id=1, source_target_pairs={{0,2},{2,4},{4,6},{6,8},{8,10},{10,12},{12,14},{14,16},{16,18},{18... | collective-permute-start | bytes 3538952 | tf_op jit(solution)/shard_map/ppermute | solution.py:14
  229.8 3.2 fusion
  233.1 3.8 fusion.30
  236.9 32.9 %collective-permute-done.3 = bf16[384,1536]{1,0:T(8,128)(2,1)} collective-permute-done((bf16[384,1536]{1,0:T(8,128)(2,1)}, bf16[384,1536]{1,0:T(8,128)(2,1)}, u32[]{:S(2)}, u32[]{:S(2)}) %collective-permute-start.3) | collective-permute-done | bytes 1179680 | tf_op jit(solution)/shard_map/ppermute | solution.py:14
  271.0 2.4 copy.61
  274.9 3.1 fusion.1
  278.1 3.7 fusion.28
  283.1 2.4 copy.66
  286.8 3.1 fusion.2
  289.9 3.8 fusion.26
  293.7 42.5 %collective-permute-done.7 = bf16[384,1536]{1,0:T(8,128)(2,1)} collective-permute-done((bf16[384,1536]{1,0:T(8,128)(2,1)}, bf16[384,1536]{1,0:T(8,128)(2,1)}, u32[]{:S(2)}, u32[]{:S(2)}) %collective-permute-start.7) | collective-permute-done | bytes 1179680 | tf_op jit(solution)/shard_map/ppermute | solution.py:14
  337.5 2.4 copy.71
  341.3 3.6 fusion.3
  344.9 5.4 %fusion.24 = f32[12,384,128]{1,2,0:T(8,128)} fusion(bf16[384,12,128]{0,2,1:T(8,128)(2,1)} %bitcast.844, f32[12,384,384]{1,2,0:T(8,128)S(1)} %get-tuple-element.88, f32[12,384]{1,0:T(8,128)S(1)} %get-tuple-element.87, pred[]{:T(512)} %get-tuple-element.8), kind=kOutput, calls=%fused_computation.37 | convolution fusion | flops 461832192 | bytes 10635265 | tf_op jit(solution)/shard_map/hqk,khd->hqd/dot_general | solution.py:30
  350.4 7.2 %fusion.4 = (f32[12,384]{1,0:T(8,128)}, f32[12,384,384]{1,2,0:T(8,128)}) fusion(pred[]{:T(512)} %get-tuple-element.10, bf16[384,12,128]{0,2,1:T(8,128)(2,1)S(1)} %bitcast.829, bf16[384,12,128]{0,2,1:T(8,128)(2,1)} %bitcast.21), kind=kOutput, calls=%fused_computation.18 | convolution fusion | flops 458288640 | bytes 9455617 | tf_op jit(solution)/shard_map/qhd,khd->hqk/dot_general | solution.py:23
  357.7 5.6 %fusion.8 = (f32[12,384]{1,0:T(8,128)}, f32[12,384]{1,0:T(8,128)}) fusion(f32[12,384,384]{1,2,0:T(8,128)S(1)} %bitcast.832, f32[12,384]{1,0:T(8,128)S(1)} %copy-done.41, pred[]{:T(512)} %get-tuple-element.5, f32[12,384]{1,0:T(8,128)S(1)} %copy-done.44, f32[12,384,384]{1,2,0:T(8,128)S(1)} %bitcast.834, pred[]{:T(512)} %get-tuple-element.7), kind=kLoop, calls=%fused_computation.22 | loop fusion | flops 17685504 | bytes 14229506 | tf_op jit(solution)/shard_map/reduce_sum | solution.py:29
  363.3 6.7 %fusion.5 = (f32[12,384]{1,0:T(8,128)}, f32[12,384,384]{1,2,0:T(8,128)}) fusion(pred[]{:T(512)} %get-tuple-element.9, bf16[384,12,128]{0,2,1:T(8,128)(2,1)S(1)} %bitcast.830, bf16[384,12,128]{0,2,1:T(8,128)(2,1)} %bitcast.25), kind=kOutput, calls=%fused_computation.19 | convolution fusion | flops 458288640 | bytes 9455617 | tf_op jit(solution)/shard_map/qhd,khd->hqk/dot_general | solution.py:23
  369.9 5.1 %fusion.12 = (f32[12,384]{1,0:T(8,128)}, f32[12,384]{1,0:T(8,128)}) fusion(f32[12,384,384]{1,2,0:T(8,128)S(1)} %bitcast.836, f32[12,384]{1,0:T(8,128)S(1)} %copy-done.47, pred[]{:T(512)} %get-tuple-element.6, f32[12,384]{1,0:T(8,128)S(1)} %get-tuple-element.87, f32[12,384,384]{1,2,0:T(8,128)S(1)} %get-tuple-element.88, pred[]{:T(512)} %get-tuple-element.8), kind=kLoop, calls=%fused_computation.26 | loop fusion | flops 17685504 | bytes 14229506 | tf_op jit(solution)/shard_map/reduce_sum | solution.py:29
  375.0 13.7 %collective-permute-done.9 = bf16[384,1536]{1,0:T(8,128)(2,1)} collective-permute-done((bf16[384,1536]{1,0:T(8,128)(2,1)}, bf16[384,1536]{1,0:T(8,128)(2,1)}, u32[]{:S(2)}, u32[]{:S(2)}) %collective-permute-start.9) | collective-permute-done | bytes 1179680 | tf_op jit(solution)/shard_map/ppermute | solution.py:14
  390.5 7.4 %fusion.22 = f32[12,384,128]{1,2,0:T(8,128)} fusion(bf16[384,12,128]{0,2,1:T(8,128)(2,1)S(1)} %bitcast.846, f32[12,384,384]{1,2,0:T(8,128)} %get-tuple-element.86, f32[12,384]{1,0:T(8,128)} %get-tuple-element.85, pred[]{:T(512)} %get-tuple-element.10), kind=kOutput, calls=%fused_computation.36 | convolution fusion | flops 461832192 | bytes 10635265 | tf_op jit(solution)/shard_map/hqk,khd->hqd/dot_general | solution.py:30
  399.6 5.3 %fusion.16 = (f32[12,384]{1,0:T(8,128)}, f32[12,384]{1,0:T(8,128)}) fusion(f32[12,384,384]{1,2,0:T(8,128)S(1)} %bitcast.838, f32[12,384]{1,0:T(8,128)S(1)} %copy-done.51, pred[]{:T(512)} %get-tuple-element.10, f32[12,384]{1,0:T(8,128)S(1)} %copy-done.53, f32[12,384,384]{1,2,0:T(8,128)S(1)} %copy-done.3, pred[]{:T(512)} %get-tuple-element.9), kind=kLoop, calls=%fused_computation.30 | loop fusion | flops 17685504 | bytes 14229506 | tf_op jit(solution)/shard_map/reduce_sum | solution.py:29
  407.0 6.9 %fusion.20 = f32[12,384,128]{1,2,0:T(8,128)} fusion(bf16[384,12,128]{0,2,1:T(8,128)(2,1)S(1)} %bitcast.845, f32[12,384,384]{1,2,0:T(8,128)} %get-tuple-element.84, f32[12,384]{1,0:T(8,128)} %get-tuple-element.83, pred[]{:T(512)} %get-tuple-element.9), kind=kOutput, calls=%fused_computation.35 | convolution fusion | flops 461832192 | bytes 10635265 | tf_op jit(solution)/shard_map/hqk,khd->hqd/dot_general | solution.py:30
  414.3 2.0 fusion.262
  416.3 17.8 %fusion.68 = bf16[384,12,128]{0,2,1:T(8,128)(2,1)} fusion(f32[12,384,128]{1,2,0:T(8,128)} %fusion.145, f32[12,384,128]{1,2,0:T(8,128)} %fusion.147, f32[12,384,128]{1,2,0:T(8,128)} %fusion.149, f32[12,384,128]{1,2,0:T(8,128)} %fusion.151, f32[12,384,128]{1,2,0:T(8,128)} %fusion.153, f32[12,384,128]{1,2,0:T(8,128)S(1)} %fusion.155, ...), kind=kOutput, calls=%fused_computation.77 | convolution fusion | flops 72990720 | bytes 47431712 | tf_op jit(solution)/shard_map/hqk,khd->hqd/dot_general | solution.py:30
  434.1 9.4 %convolution_convert_fusion = bf16[384,3072]{1,0:T(8,128)(2,1)} fusion(bf16[384,1536]{0,1:T(8,128)(2,1)} %bitcast.840, bf16[1536,3072]{1,0:T(8,128)(2,1)} %param.17), kind=kOutput, calls=%fused_computation.34 | convolution fusion | flops 3625058304 | bytes 12976128 | tf_op jit(solution)/shard_map/dot_general | solution.py:87
  443.5 49.9 %reduce-scatter.2.cloned.1.call-done = bf16[192,3072]{1,0:T(8,128)(2,1)} async-done(((bf16[384,3072]{1,0:T(8,128)(2,1)}), bf16[192,3072]{1,0:T(8,128)(2,1)}) %reduce-scatter.2.cloned.1.call-update) | async-done | bytes 1179664 | tf_op jit(solution)/shard_map/reduce_scatter | solution.py:86
  (285 shorter events, 63.7 us)
Async XLA Ops:
  6.5 29.5 %copy-start.7 = (bf16[384,1536]{1,0:T(8,128)(2,1)S(1)}, bf16[384,1536]{1,0:T(8,128)(2,1)}, u32[]{:S(2)}) copy-start(bf16[384,1536]{1,0:T(8,128)(2,1)} %param.9) | copy-start | bytes 3538948
  6.5 486.9 %reduce-scatter.2.cloned.1.call-start = ((), (), s32[]{:S(2)}) async-start(), calls=%async_computation.1 | async-start | bytes 3538944 | tf_op jit(solution)/shard_map/reduce_scatter | solution.py:86
  6.5 86.5 %collective-permute-start.30 = (bf16[32,1536]{1,0:T(8,128)(2,1)}, bf16[32,1536]{1,0:T(8,128)(2,1)}, u32[]{:S(2)}, u32[]{:S(2)}) collective-permute-start(bf16[32,1536]{1,0:T(8,128)(2,1)} %param.12), channel_id=1, source_target_pairs={{8,0},{10,2},{12,4},{14,6},{16,8},{18,10},{20,12},{22,14},{24,16},... | collective-permute-start | bytes 294920 | tf_op jit(solution)/shard_map/ppermute | solution.py:14
  8.0 82.5 %collective-permute-start.28 = (bf16[32,1536]{1,0:T(8,128)(2,1)}, bf16[32,1536]{1,0:T(8,128)(2,1)}, u32[]{:S(2)}, u32[]{:S(2)}) collective-permute-start(bf16[32,1536]{1,0:T(8,128)(2,1)} %param.12), channel_id=1, source_target_pairs={{6,0},{8,2},{10,4},{12,6},{14,8},{16,10},{18,12},{20,14},{22,16},{... | collective-permute-start | bytes 294920 | tf_op jit(solution)/shard_map/ppermute | solution.py:14
  9.3 78.6 %collective-permute-start.26 = (bf16[32,1536]{1,0:T(8,128)(2,1)}, bf16[32,1536]{1,0:T(8,128)(2,1)}, u32[]{:S(2)}, u32[]{:S(2)}) collective-permute-start(bf16[32,1536]{1,0:T(8,128)(2,1)} %param.12), channel_id=1, source_target_pairs={{4,0},{6,2},{8,4},{10,6},{12,8},{14,10},{16,12},{18,14},{20,16},{2... | collective-permute-start | bytes 294920 | tf_op jit(solution)/shard_map/ppermute | solution.py:14
  10.6 74.7 %collective-permute-start.24 = (bf16[32,1536]{1,0:T(8,128)(2,1)}, bf16[32,1536]{1,0:T(8,128)(2,1)}, u32[]{:S(2)}, u32[]{:S(2)}) collective-permute-start(bf16[32,1536]{1,0:T(8,128)(2,1)} %param.12), channel_id=1, source_target_pairs={{2,0},{4,2},{6,4},{8,6},{10,8},{12,10},{14,12},{16,14},{18,16},{20... | collective-permute-start | bytes 294920 | tf_op jit(solution)/shard_map/ppermute | solution.py:14
  11.9 37.0 %collective-permute-start.12 = (bf16[32,1536]{1,0:T(8,128)(2,1)}, bf16[32,1536]{1,0:T(8,128)(2,1)}, u32[]{:S(2)}, u32[]{:S(2)}) collective-permute-start(bf16[32,1536]{1,0:T(8,128)(2,1)} %param.12), channel_id=1, source_target_pairs={{0,12},{2,14},{4,16},{6,18},{8,20},{10,22},{12,24},{14,26},{16,28}... | collective-permute-start | bytes 294920 | tf_op jit(solution)/shard_map/ppermute | solution.py:14
  48.8 18.4 %copy-start.81 = (pred[32]{0:T(512)(128)(4,1)S(1)}, pred[32]{0:T(512)(128)(4,1)}, u32[]{:S(2)}) copy-start(pred[32]{0:T(512)(128)(4,1)} %compare_and_fusion.10) | copy-start | bytes 100
  48.8 7.2 %collective-permute-start.14 = (bf16[32,1536]{1,0:T(8,128)(2,1)S(1)}, bf16[32,1536]{1,0:T(8,128)(2,1)S(1)}, u32[]{:S(2)}, u32[]{:S(2)}) collective-permute-start(bf16[32,1536]{1,0:T(8,128)(2,1)S(1)} %copy-done.75), channel_id=1, source_target_pairs={{0,10},{2,12},{4,14},{6,16},{8,18},{10,20},{12,22},{14,24},{16,26}... | collective-permute-start | bytes 294920 | tf_op jit(solution)/shard_map/ppermute | solution.py:14
  55.1 134.2 %copy-start.14 = (f32[12,384]{1,0:T(8,128)}, f32[12,384]{1,0:T(8,128)S(1)}, u32[]{:S(2)}) copy-start(f32[12,384]{1,0:T(8,128)S(1)} %get-tuple-element.81) | copy-start | bytes 55300
  55.1 18.2 %copy-start.80 = (pred[32]{0:T(512)(128)(4,1)S(1)}, pred[32]{0:T(512)(128)(4,1)}, u32[]{:S(2)}) copy-start(pred[32]{0:T(512)(128)(4,1)} %compare_and_fusion.9) | copy-start | bytes 100
  56.1 6.3 %collective-permute-start.16 = (bf16[32,1536]{1,0:T(8,128)(2,1)S(1)}, bf16[32,1536]{1,0:T(8,128)(2,1)S(1)}, u32[]{:S(2)}, u32[]{:S(2)}) collective-permute-start(bf16[32,1536]{1,0:T(8,128)(2,1)S(1)} %copy-done.75), channel_id=1, source_target_pairs={{0,8},{2,10},{4,12},{6,14},{8,16},{10,18},{12,20},{14,22},{16,24},... | collective-permute-start | bytes 294920 | tf_op jit(solution)/shard_map/ppermute | solution.py:14
  60.5 123.7 %copy-start.16 = (f32[12,384]{1,0:T(8,128)}, f32[12,384]{1,0:T(8,128)S(1)}, u32[]{:S(2)}) copy-start(f32[12,384]{1,0:T(8,128)S(1)} %get-tuple-element.79) | copy-start | bytes 55300
  60.5 20.9 %copy-start.79 = (pred[32]{0:T(512)(128)(4,1)S(1)}, pred[32]{0:T(512)(128)(4,1)}, u32[]{:S(2)}) copy-start(pred[32]{0:T(512)(128)(4,1)} %compare_and_fusion.8) | copy-start | bytes 100
  62.4 7.0 %collective-permute-start.18 = (bf16[32,1536]{1,0:T(8,128)(2,1)S(1)}, bf16[32,1536]{1,0:T(8,128)(2,1)S(1)}, u32[]{:S(2)}, u32[]{:S(2)}) collective-permute-start(bf16[32,1536]{1,0:T(8,128)(2,1)S(1)} %copy-done.75), channel_id=1, source_target_pairs={{0,6},{2,8},{4,10},{6,12},{8,14},{10,16},{12,18},{14,20},{16,22},{... | collective-permute-start | bytes 294920 | tf_op jit(solution)/shard_map/ppermute | solution.py:14
  67.5 52.5 %copy-start.18 = (f32[12,384]{1,0:T(8,128)}, f32[12,384]{1,0:T(8,128)S(1)}, u32[]{:S(2)}) copy-start(f32[12,384]{1,0:T(8,128)S(1)} %get-tuple-element.77) | copy-start | bytes 55300
  67.6 17.4 %copy-start.78 = (pred[32]{0:T(512)(128)(4,1)S(1)}, pred[32]{0:T(512)(128)(4,1)}, u32[]{:S(2)}) copy-start(pred[32]{0:T(512)(128)(4,1)} %compare_and_fusion.7) | copy-start | bytes 100
  69.4 6.1 %collective-permute-start.20 = (bf16[32,1536]{1,0:T(8,128)(2,1)S(1)}, bf16[32,1536]{1,0:T(8,128)(2,1)S(1)}, u32[]{:S(2)}, u32[]{:S(2)}) collective-permute-start(bf16[32,1536]{1,0:T(8,128)(2,1)S(1)} %copy-done.75), channel_id=1, source_target_pairs={{0,4},{2,6},{4,8},{6,10},{8,12},{10,14},{12,16},{14,18},{16,20},{1... | collective-permute-start | bytes 294920 | tf_op jit(solution)/shard_map/ppermute | solution.py:14
  73.7 53.9 %copy-start.20 = (f32[12,384]{1,0:T(8,128)}, f32[12,384]{1,0:T(8,128)S(1)}, u32[]{:S(2)}) copy-start(f32[12,384]{1,0:T(8,128)S(1)} %get-tuple-element.75) | copy-start | bytes 55300
  73.7 12.9 %copy-start.77 = (pred[32]{0:T(512)(128)(4,1)S(1)}, pred[32]{0:T(512)(128)(4,1)}, u32[]{:S(2)}) copy-start(pred[32]{0:T(512)(128)(4,1)} %compare_and_fusion.5) | copy-start | bytes 100
  75.5 8.1 %collective-permute-start.22 = (bf16[32,1536]{1,0:T(8,128)(2,1)S(1)}, bf16[32,1536]{1,0:T(8,128)(2,1)S(1)}, u32[]{:S(2)}, u32[]{:S(2)}) collective-permute-start(bf16[32,1536]{1,0:T(8,128)(2,1)S(1)} %copy-done.75), channel_id=1, source_target_pairs={{0,2},{2,4},{4,6},{6,8},{8,10},{10,12},{12,14},{14,16},{16,18},{18... | collective-permute-start | bytes 294920 | tf_op jit(solution)/shard_map/ppermute | solution.py:14
  81.8 51.9 %copy-start.22 = (f32[12,384]{1,0:T(8,128)}, f32[12,384]{1,0:T(8,128)S(1)}, u32[]{:S(2)}) copy-start(f32[12,384]{1,0:T(8,128)S(1)} %get-tuple-element.73) | copy-start | bytes 55300
  83.6 14.4 %collective-permute-start.34 = (bf16[32,1536]{1,0:T(8,128)(2,1)S(1)}, bf16[32,1536]{1,0:T(8,128)(2,1)S(1)}, u32[]{:S(2)}, u32[]{:S(2)}) collective-permute-start(bf16[32,1536]{1,0:T(8,128)(2,1)S(1)} %copy-done.75), channel_id=1, source_target_pairs={{12,0},{14,2},{16,4},{18,6},{20,8},{22,10},{24,12},{26,14},{28,16}... | collective-permute-start | bytes 294920 | tf_op jit(solution)/shard_map/ppermute | solution.py:14
  85.3 59.0 %copy-start.24 = (f32[12,384]{1,0:T(8,128)}, f32[12,384]{1,0:T(8,128)S(1)}, u32[]{:S(2)}) copy-start(f32[12,384]{1,0:T(8,128)S(1)} %get-tuple-element.71) | copy-start | bytes 55300
  85.3 11.1 %collective-permute-start.32 = (bf16[32,1536]{1,0:T(8,128)(2,1)S(1)}, bf16[32,1536]{1,0:T(8,128)(2,1)S(1)}, u32[]{:S(2)}, u32[]{:S(2)}) collective-permute-start(bf16[32,1536]{1,0:T(8,128)(2,1)S(1)} %copy-done.75), channel_id=1, source_target_pairs={{10,0},{12,2},{14,4},{16,6},{18,8},{20,10},{22,12},{24,14},{26,16}... | collective-permute-start | bytes 294920 | tf_op jit(solution)/shard_map/ppermute | solution.py:14
  87.8 64.8 %copy-start.26 = (f32[12,384]{1,0:T(8,128)}, f32[12,384]{1,0:T(8,128)S(1)}, u32[]{:S(2)}) copy-start(f32[12,384]{1,0:T(8,128)S(1)} %get-tuple-element.67) | copy-start | bytes 55300
  87.9 73.6 %collective-permute-start.31 = (bf16[32,1536]{1,0:T(8,128)(2,1)}, bf16[32,1536]{1,0:T(8,128)(2,1)S(1)}, u32[]{:S(2)}, u32[]{:S(2)}) collective-permute-start(bf16[32,1536]{1,0:T(8,128)(2,1)} %param.13), channel_id=1, source_target_pairs={{8,0},{10,2},{12,4},{14,6},{16,8},{18,10},{20,12},{22,14},{24,16},... | collective-permute-start | bytes 294920 | tf_op jit(solution)/shard_map/ppermute | solution.py:14
  90.4 66.2 %copy-start.28 = (f32[12,384]{1,0:T(8,128)}, f32[12,384]{1,0:T(8,128)S(1)}, u32[]{:S(2)}) copy-start(f32[12,384]{1,0:T(8,128)S(1)} %get-tuple-element.65) | copy-start | bytes 55300
  90.4 67.0 %collective-permute-start.29 = (bf16[32,1536]{1,0:T(8,128)(2,1)}, bf16[32,1536]{1,0:T(8,128)(2,1)S(1)}, u32[]{:S(2)}, u32[]{:S(2)}) collective-permute-start(bf16[32,1536]{1,0:T(8,128)(2,1)} %param.13), channel_id=1, source_target_pairs={{6,0},{8,2},{10,4},{12,6},{14,8},{16,10},{18,12},{20,14},{22,16},{... | collective-permute-start | bytes 294920 | tf_op jit(solution)/shard_map/ppermute | solution.py:14
  93.0 67.7 %copy-start.30 = (f32[12,384]{1,0:T(8,128)}, f32[12,384]{1,0:T(8,128)S(1)}, u32[]{:S(2)}) copy-start(f32[12,384]{1,0:T(8,128)S(1)} %get-tuple-element.63) | copy-start | bytes 55300
  93.0 16.1 %copy-start.83 = (pred[32]{0:T(512)(128)(4,1)S(1)}, pred[32]{0:T(512)(128)(4,1)}, u32[]{:S(2)}) copy-start(pred[32]{0:T(512)(128)(4,1)} %compare_and_fusion) | copy-start | bytes 100
  93.0 60.4 %collective-permute-start.27 = (bf16[32,1536]{1,0:T(8,128)(2,1)}, bf16[32,1536]{1,0:T(8,128)(2,1)S(1)}, u32[]{:S(2)}, u32[]{:S(2)}) collective-permute-start(bf16[32,1536]{1,0:T(8,128)(2,1)} %param.13), channel_id=1, source_target_pairs={{4,0},{6,2},{8,4},{10,6},{12,8},{14,10},{16,12},{18,14},{20,16},{2... | collective-permute-start | bytes 294920 | tf_op jit(solution)/shard_map/ppermute | solution.py:14
  95.5 73.5 %copy-start.32 = (f32[12,384]{1,0:T(8,128)}, f32[12,384]{1,0:T(8,128)S(1)}, u32[]{:S(2)}) copy-start(f32[12,384]{1,0:T(8,128)S(1)} %get-tuple-element.61) | copy-start | bytes 55300
  96.4 48.6 %collective-permute-start.25 = (bf16[32,1536]{1,0:T(8,128)(2,1)}, bf16[32,1536]{1,0:T(8,128)(2,1)S(1)}, u32[]{:S(2)}, u32[]{:S(2)}) collective-permute-start(bf16[32,1536]{1,0:T(8,128)(2,1)} %param.13), channel_id=1, source_target_pairs={{2,0},{4,2},{6,4},{8,6},{10,8},{12,10},{14,12},{16,14},{18,16},{20... | collective-permute-start | bytes 294920 | tf_op jit(solution)/shard_map/ppermute | solution.py:14
  98.0 81.2 %copy-start.34 = (f32[12,384]{1,0:T(8,128)}, f32[12,384]{1,0:T(8,128)S(1)}, u32[]{:S(2)}) copy-start(f32[12,384]{1,0:T(8,128)S(1)} %get-tuple-element.59) | copy-start | bytes 55300
  98.0 13.5 %collective-permute-start.17 = (bf16[32,1536]{1,0:T(8,128)(2,1)}, bf16[32,1536]{1,0:T(8,128)(2,1)S(1)}, u32[]{:S(2)}, u32[]{:S(2)}) collective-permute-start(bf16[32,1536]{1,0:T(8,128)(2,1)} %param.13), channel_id=1, source_target_pairs={{0,8},{2,10},{4,12},{6,14},{8,16},{10,18},{12,20},{14,22},{16,24},... | collective-permute-start | bytes 294920 | tf_op jit(solution)/shard_map/ppermute | solution.py:14
  109.4 81.8 %copy-start.4 = (f32[12,384,32]{1,2,0:T(8,128)}, f32[12,384,32]{1,2,0:T(8,128)S(1)}, u32[]{:S(2)}) copy-start(f32[12,384,32]{1,2,0:T(8,128)S(1)} %get-tuple-element.98) | copy-start | bytes 1769476
  109.4 81.8 %copy-start.38 = (f32[12,384]{1,0:T(8,128)}, f32[12,384]{1,0:T(8,128)S(1)}, u32[]{:S(2)}) copy-start(f32[12,384]{1,0:T(8,128)S(1)} %get-tuple-element.97) | copy-start | bytes 55300
  111.5 9.3 %collective-permute-start.19 = (bf16[32,1536]{1,0:T(8,128)(2,1)}, bf16[32,1536]{1,0:T(8,128)(2,1)S(1)}, u32[]{:S(2)}, u32[]{:S(2)}) collective-permute-start(bf16[32,1536]{1,0:T(8,128)(2,1)} %param.13), channel_id=1, source_target_pairs={{0,6},{2,8},{4,10},{6,12},{8,14},{10,16},{12,18},{14,20},{16,22},{... | collective-permute-start | bytes 294920 | tf_op jit(solution)/shard_map/ppermute | solution.py:14
  120.8 7.5 %collective-permute-start.21 = (bf16[32,1536]{1,0:T(8,128)(2,1)}, bf16[32,1536]{1,0:T(8,128)(2,1)S(1)}, u32[]{:S(2)}, u32[]{:S(2)}) collective-permute-start(bf16[32,1536]{1,0:T(8,128)(2,1)} %param.13), channel_id=1, source_target_pairs={{0,4},{2,6},{4,8},{6,10},{8,12},{10,14},{12,16},{14,18},{16,20},{1... | collective-permute-start | bytes 294920 | tf_op jit(solution)/shard_map/ppermute | solution.py:14
  128.3 6.1 %collective-permute-start.23 = (bf16[32,1536]{1,0:T(8,128)(2,1)}, bf16[32,1536]{1,0:T(8,128)(2,1)S(1)}, u32[]{:S(2)}, u32[]{:S(2)}) collective-permute-start(bf16[32,1536]{1,0:T(8,128)(2,1)} %param.13), channel_id=1, source_target_pairs={{0,2},{2,4},{4,6},{6,8},{8,10},{10,12},{12,14},{14,16},{16,18},{18... | collective-permute-start | bytes 294920 | tf_op jit(solution)/shard_map/ppermute | solution.py:14
  134.5 46.3 %collective-permute-start.15 = (bf16[32,1536]{1,0:T(8,128)(2,1)}, bf16[32,1536]{1,0:T(8,128)(2,1)S(1)}, u32[]{:S(2)}, u32[]{:S(2)}) collective-permute-start(bf16[32,1536]{1,0:T(8,128)(2,1)} %param.13), channel_id=1, source_target_pairs={{0,10},{2,12},{4,14},{6,16},{8,18},{10,20},{12,22},{14,24},{16,26}... | collective-permute-start | bytes 294920 | tf_op jit(solution)/shard_map/ppermute | solution.py:14
  145.0 42.0 %collective-permute-start.13 = (bf16[32,1536]{1,0:T(8,128)(2,1)}, bf16[32,1536]{1,0:T(8,128)(2,1)S(1)}, u32[]{:S(2)}, u32[]{:S(2)}) collective-permute-start(bf16[32,1536]{1,0:T(8,128)(2,1)} %param.13), channel_id=1, source_target_pairs={{0,12},{2,14},{4,16},{6,18},{8,20},{10,22},{12,24},{14,26},{16,28}... | collective-permute-start | bytes 294920 | tf_op jit(solution)/shard_map/ppermute | solution.py:14
  153.4 262.9 %collective-permute-start.35 = (bf16[32,1536]{1,0:T(8,128)(2,1)}, bf16[32,1536]{1,0:T(8,128)(2,1)}, u32[]{:S(2)}, u32[]{:S(2)}) collective-permute-start(bf16[32,1536]{1,0:T(8,128)(2,1)} %param.13), channel_id=1, source_target_pairs={{12,0},{14,2},{16,4},{18,6},{20,8},{22,10},{24,12},{26,14},{28,16}... | collective-permute-start | bytes 294920 | tf_op jit(solution)/shard_map/ppermute | solution.py:14
  157.4 12.4 %collective-permute-start.33 = (bf16[32,1536]{1,0:T(8,128)(2,1)}, bf16[32,1536]{1,0:T(8,128)(2,1)S(1)}, u32[]{:S(2)}, u32[]{:S(2)}) collective-permute-start(bf16[32,1536]{1,0:T(8,128)(2,1)} %param.13), channel_id=1, source_target_pairs={{10,0},{12,2},{14,4},{16,6},{18,8},{20,10},{22,12},{24,14},{26,16}... | collective-permute-start | bytes 294920 | tf_op jit(solution)/shard_map/ppermute | solution.py:14
  161.4 59.3 %collective-permute-start = (bf16[384,1536]{0,1:T(8,128)(2,1)}, bf16[384,1536]{0,1:T(8,128)(2,1)}, u32[]{:S(2)}, u32[]{:S(2)}) collective-permute-start(bf16[384,1536]{0,1:T(8,128)(2,1)} %copy.48), channel_id=1, source_target_pairs={{0,6},{2,8},{4,10},{6,12},{8,14},{10,16},{12,18},{14,20},{16,22},{... | collective-permute-start | bytes 3538952 | tf_op jit(solution)/shard_map/ppermute | solution.py:14
  169.8 46.2 %collective-permute-start.1 = (bf16[384,1536]{1,0:T(8,128)(2,1)}, bf16[384,1536]{1,0:T(8,128)(2,1)}, u32[]{:S(2)}, u32[]{:S(2)}) collective-permute-start(bf16[384,1536]{1,0:T(8,128)(2,1)} %param.11), channel_id=1, source_target_pairs={{0,6},{2,8},{4,10},{6,12},{8,14},{10,16},{12,18},{14,20},{16,22},{... | collective-permute-start | bytes 3538952 | tf_op jit(solution)/shard_map/ppermute | solution.py:14
  180.8 92.7 %collective-permute-start.2 = (bf16[384,1536]{0,1:T(8,128)(2,1)}, bf16[384,1536]{0,1:T(8,128)(2,1)}, u32[]{:S(2)}, u32[]{:S(2)}) collective-permute-start(bf16[384,1536]{0,1:T(8,128)(2,1)} %copy.48), channel_id=1, source_target_pairs={{0,4},{2,6},{4,8},{6,10},{8,12},{10,14},{12,16},{14,18},{16,20},{1... | collective-permute-start | bytes 3538952 | tf_op jit(solution)/shard_map/ppermute | solution.py:14
  187.0 82.8 %collective-permute-start.3 = (bf16[384,1536]{1,0:T(8,128)(2,1)}, bf16[384,1536]{1,0:T(8,128)(2,1)}, u32[]{:S(2)}, u32[]{:S(2)}) collective-permute-start(bf16[384,1536]{1,0:T(8,128)(2,1)} %param.11), channel_id=1, source_target_pairs={{0,4},{2,6},{4,8},{6,10},{8,12},{10,14},{12,16},{14,18},{16,20},{1... | collective-permute-start | bytes 3538952 | tf_op jit(solution)/shard_map/ppermute | solution.py:14
  216.0 69.5 %collective-permute-start.4 = (bf16[384,1536]{0,1:T(8,128)(2,1)}, bf16[384,1536]{0,1:T(8,128)(2,1)}, u32[]{:S(2)}, u32[]{:S(2)}) collective-permute-start(bf16[384,1536]{0,1:T(8,128)(2,1)} %copy.48), channel_id=1, source_target_pairs={{0,2},{2,4},{4,6},{6,8},{8,10},{10,12},{12,14},{14,16},{16,18},{18... | collective-permute-start | bytes 3538952 | tf_op jit(solution)/shard_map/ppermute | solution.py:14
  220.8 61.0 %collective-permute-start.5 = (bf16[384,1536]{1,0:T(8,128)(2,1)}, bf16[384,1536]{1,0:T(8,128)(2,1)}, u32[]{:S(2)}, u32[]{:S(2)}) collective-permute-start(bf16[384,1536]{1,0:T(8,128)(2,1)} %param.11), channel_id=1, source_target_pairs={{0,2},{2,4},{4,6},{6,8},{8,10},{10,12},{12,14},{14,16},{16,18},{18... | collective-permute-start | bytes 3538952 | tf_op jit(solution)/shard_map/ppermute | solution.py:14
  269.7 70.2 %collective-permute-start.6 = (bf16[384,1536]{0,1:T(8,128)(2,1)}, bf16[384,1536]{0,1:T(8,128)(2,1)}, u32[]{:S(2)}, u32[]{:S(2)}) collective-permute-start(bf16[384,1536]{0,1:T(8,128)(2,1)} %copy.48), channel_id=1, source_target_pairs={{2,0},{4,2},{6,4},{8,6},{10,8},{12,10},{14,12},{16,14},{18,16},{20... | collective-permute-start | bytes 3538952 | tf_op jit(solution)/shard_map/ppermute | solution.py:14
  273.4 62.8 %collective-permute-start.7 = (bf16[384,1536]{1,0:T(8,128)(2,1)}, bf16[384,1536]{1,0:T(8,128)(2,1)}, u32[]{:S(2)}, u32[]{:S(2)}) collective-permute-start(bf16[384,1536]{1,0:T(8,128)(2,1)} %param.11), channel_id=1, source_target_pairs={{2,0},{4,2},{6,4},{8,6},{10,8},{12,10},{14,12},{16,14},{18,16},{20... | collective-permute-start | bytes 3538952 | tf_op jit(solution)/shard_map/ppermute | solution.py:14
  281.8 81.5 %collective-permute-start.10 = (bf16[384,1536]{0,1:T(8,128)(2,1)}, bf16[384,1536]{0,1:T(8,128)(2,1)}, u32[]{:S(2)}, u32[]{:S(2)}) collective-permute-start(bf16[384,1536]{0,1:T(8,128)(2,1)} %copy.48), channel_id=1, source_target_pairs={{6,0},{8,2},{10,4},{12,6},{14,8},{16,10},{18,12},{20,14},{22,16},{... | collective-permute-start | bytes 3538952 | tf_op jit(solution)/shard_map/ppermute | solution.py:14
  285.5 64.9 %collective-permute-start.8 = (bf16[384,1536]{0,1:T(8,128)(2,1)}, bf16[384,1536]{0,1:T(8,128)(2,1)}, u32[]{:S(2)}, u32[]{:S(2)}) collective-permute-start(bf16[384,1536]{0,1:T(8,128)(2,1)} %copy.48), channel_id=1, source_target_pairs={{4,0},{6,2},{8,4},{10,6},{12,8},{14,10},{16,12},{18,14},{20,16},{2... | collective-permute-start | bytes 3538952 | tf_op jit(solution)/shard_map/ppermute | solution.py:14
  336.2 68.6 %collective-permute-start.11 = (bf16[384,1536]{1,0:T(8,128)(2,1)}, bf16[384,1536]{1,0:T(8,128)(2,1)}, u32[]{:S(2)}, u32[]{:S(2)}) collective-permute-start(bf16[384,1536]{1,0:T(8,128)(2,1)} %param.11), channel_id=1, source_target_pairs={{6,0},{8,2},{10,4},{12,6},{14,8},{16,10},{18,12},{20,14},{22,16},{... | collective-permute-start | bytes 3538952 | tf_op jit(solution)/shard_map/ppermute | solution.py:14
  340.0 48.8 %collective-permute-start.9 = (bf16[384,1536]{1,0:T(8,128)(2,1)}, bf16[384,1536]{1,0:T(8,128)(2,1)}, u32[]{:S(2)}, u32[]{:S(2)}) collective-permute-start(bf16[384,1536]{1,0:T(8,128)(2,1)} %param.11), channel_id=1, source_target_pairs={{4,0},{6,2},{8,4},{10,6},{12,8},{14,10},{16,12},{18,14},{20,16},{2... | collective-permute-start | bytes 3538952 | tf_op jit(solution)/shard_map/ppermute | solution.py:14
  341.3 16.4 %slice-start = ((s8[7077888]{0:T(1024)(128)(4,1)}), s8[4194304]{0:T(1024)(128)(4,1)S(1)}, s32[]{:S(2)}) async-start(s8[7077888]{0:T(1024)(128)(4,1)} %bitcast.831), calls=%async_computation.2 | async-start | bytes 8388608
  341.3 16.3 %slice-start.2 = ((s8[7077888]{0:T(1024)(128)(4,1)}), s8[4194304]{0:T(1024)(128)(4,1)S(1)}, s32[]{:S(2)}) async-start(s8[7077888]{0:T(1024)(128)(4,1)} %bitcast.833), calls=%async_computation.4 | async-start | bytes 8388608
  344.9 25.0 %copy-start.49 = (f32[12,384]{1,0:T(8,128)}, f32[12,384]{1,0:T(8,128)S(1)}, u32[]{:S(2)}) copy-start(f32[12,384]{1,0:T(8,128)S(1)} %get-tuple-element.87) | copy-start | bytes 55300
  344.9 12.7 %slice-start.1 = ((s8[7077888]{0:T(1024)(128)(4,1)}), s8[2883584]{0:T(1024)(128)(4,1)S(1)}, s32[]{:S(2)}) async-start(s8[7077888]{0:T(1024)(128)(4,1)} %bitcast.831), calls=%async_computation.3 | async-start | bytes 5767168
  344.9 12.7 %slice-start.3 = ((s8[7077888]{0:T(1024)(128)(4,1)}), s8[2883584]{0:T(1024)(128)(4,1)S(1)}, s32[]{:S(2)}) async-start(s8[7077888]{0:T(1024)(128)(4,1)} %bitcast.833), calls=%async_computation.5 | async-start | bytes 5767168
  350.4 19.6 %slice-start.4 = ((s8[7077888]{0:T(1024)(128)(4,1)}), s8[4194304]{0:T(1024)(128)(4,1)S(1)}, s32[]{:S(2)}) async-start(s8[7077888]{0:T(1024)(128)(4,1)} %bitcast.835), calls=%async_computation.6 | async-start | bytes 8388608
  357.7 12.3 %slice-start.5 = ((s8[7077888]{0:T(1024)(128)(4,1)}), s8[2883584]{0:T(1024)(128)(4,1)S(1)}, s32[]{:S(2)}) async-start(s8[7077888]{0:T(1024)(128)(4,1)} %bitcast.835), calls=%async_computation.7 | async-start | bytes 5767168
  (65 other events, 420.3 us)
Sparse Core Ops, SparseCore 0:
  443.6 49.7 reduce-scatter.1
where the time goes:
time: 511 us; the launch traced here: 501 us
  waiting for transfers between devices  174 us (34%)
  starting transfers between devices  128 us (25%)
  matrix products  122 us (24%)
  other arithmetic  39.8 us (8%)
  local copies, waits for them, and re-layouts  18.9 us (4%)
  between operations  17.4 us (3%)
    ppermute x36, starting transfers between devices, passed_along(): return lax.ppermute(shard, axis, pairs)  128 us
    ppermute x36, waiting for transfers between devices, passed_along(): return lax.ppermute(shard, axis, pairs)  124 us
    dot_general x20, matrix products, attend(): jnp.einsum('hqk,khd->hqd', weight.astype(jnp.bfloat16), v_heads, preferre...  74.6 us
    reduce_scatter x1, waiting for transfers between devices, body(): lax.psum_scatter(jnp.dot(attended, out_weight, preferred_element_type=jnp...  49.9 us
    dot_general x20, matrix products, attend(): jnp.einsum('qhd,khd->hqk', q_heads, k_heads, preferred_element_type=jnp.f...  38.2 us
    reduce_sum x17, other arithmetic, attend(): total = jnp.sum(weight, axis=-1)  27.5 us
    ppermute x6, local copies, waits for them, and re-layouts, passed_along(): return lax.ppermute(shard, axis, pairs)  13 us
  transfers between devices with their start and end apart: 37, of which 12 were waited for; matrix products, arithmetic and copies ran while one was open for 31% of the time, Pallas kernels for 0%

commit v1 on v0

v1 whole, which is shorter than its diff:
```python
import functools

import jax
import jax.numpy as jnp
from jax import lax
from jax.experimental import pallas as pl
from jax.experimental.pallas import tpu as pltpu
from jax.sharding import PartitionSpec as P

HD = 128
MOST = 7
SPAN = 2 * MOST - 1
GROUP = 3
LOW = -1e30
MESH = pl.DeviceIdType.MESH


def kernel(
    n_seq,
    n_head,
    near_ref,
    clip_ref,
    text_ref,
    q_hbm,
    k_hbm,
    v_hbm,
    tk_hbm,
    tv_hbm,
    w_hbm,
    out_ref,
    q,
    kv,
    text,
    stage,
    w,
    acc,
    top,
    total,
    attended,
    partial,
    arrived,
    near_send,
    near_recv,
    far_send,
    far_recv,
    text_send,
    text_recv,
    out_send,
    out_recv,
    local_sem,
):
    me = lax.axis_index("seq")
    head = lax.axis_index("head")
    rows, width = q.shape
    heads = width // HD
    group = GROUP if heads % GROUP == 0 else 1
    chunks = heads // group
    cw = group * HD
    trows = tk_hbm.shape[0]
    text_pad = text.shape[1]

    def exists(by):
        return (me + by >= 0) & (me + by < n_seq)

    def near_slot(by):
        return 1 if by == 1 else 2

    def far_slot(by):
        return 3 if by == 2 else 4

    own_copies = [
        pltpu.make_async_copy(q_hbm, q, local_sem.at[0]),
        pltpu.make_async_copy(k_hbm, kv.at[0, pl.ds(0, rows)], local_sem.at[1]),
        pltpu.make_async_copy(v_hbm, kv.at[1, pl.ds(0, rows)], local_sem.at[2]),
        pltpu.make_async_copy(tk_hbm, text.at[0, pl.ds((MOST - 1) * trows, trows)], local_sem.at[3]),
        pltpu.make_async_copy(tv_hbm, text.at[1, pl.ds((MOST - 1) * trows, trows)], local_sem.at[4]),
    ]
    w_copy = pltpu.make_async_copy(w_hbm, w, local_sem.at[5])
    text[...] = jnp.zeros_like(text)
    for copy in own_copies:
        copy.start()
    w_copy.start()
    for by in (1, -1):
        for slot, step in ((near_slot(by), by), (far_slot(by * 2), by * 2)):

            @pl.when(jnp.logical_not(exists(-step)))
            def _():
                kv[:, pl.ds(slot * rows, rows), :] = jnp.zeros((2, rows, width), kv.dtype)

    barrier = pltpu.get_barrier_semaphore()
    partners = n_head - 1
    for by in (1, -1, 2, -2):
        partners = partners + exists(by).astype(jnp.int32)

        @pl.when(exists(by))
        def _():
            pl.semaphore_signal(barrier, inc=1, device_id={"seq": me + by}, device_id_type=MESH)

    for d in range(1, n_head):
        pl.semaphore_signal(
            barrier, inc=1, device_id={"head": lax.rem(head + d, n_head)}, device_id_type=MESH
        )
    pl.semaphore_wait(barrier, partners)

    def near_copy(by, c, j):
        src = k_hbm if j == 0 else v_hbm
        i = 0 if by == 1 else 1
        return pltpu.make_async_remote_copy(
            src_ref=src.at[:, pl.ds(c * cw, cw)],
            dst_ref=kv.at[j, pl.ds(near_slot(by) * rows, rows), pl.ds(c * cw, cw)],
            send_sem=near_send.at[i, c, j],
            recv_sem=near_recv.at[i, c, j],
            device_id={"seq": me + by},
            device_id_type=MESH,
        )

    def far_copy(by, c, j):
        i = 0 if by == 2 else 1
        return pltpu.make_async_remote_copy(
            src_ref=stage.at[i, j, :, pl.ds(c * cw, cw)],
            dst_ref=kv.at[j, pl.ds(far_slot(by) * rows, rows), pl.ds(c * cw, cw)],
            send_sem=far_send.at[i, c, j],
            recv_sem=far_recv.at[i, c, j],
            device_id={"seq": me + by},
            device_id_type=MESH,
        )

    def text_copy(by, step, j):
        i = 0 if by == 1 else 1
        at = (MOST - 1) - by * (step - 1)
        return pltpu.make_async_remote_copy(
            src_ref=text.at[j, pl.ds(at * trows, trows)],
            dst_ref=text.at[j, pl.ds((at - by) * trows, trows)],
            send_sem=text_send.at[i, step - 1, j],
            recv_sem=text_recv.at[i, step - 1, j],
            device_id={"seq": me + by},
            device_id_type=MESH,
        )

    def text_start(step):
        for by in (1, -1):

            @pl.when(exists(by) & exists(-by * (step - 1)))
            def _():
                for j in range(2):
                    text_copy(by, step, j).start()

    def text_arrive(step):
        for by in (1, -1):

            @pl.when(exists(-by * step))
            def _():
                for j in range(2):
                    text_copy(by, step, j).wait_recv()

    for copy in own_copies[3:]:
        copy.wait()
    text_start(1)
    for c in range(chunks):
        for by in (1, -1):

            @pl.when(exists(by))
            def _():
                for j in range(2):
                    near_copy(by, c, j).start()

    def listed(tile):
        found = near_ref[0, 0] == tile
        for i in range(1, near_ref.shape[1]):
            found = found | (near_ref[0, i] == tile)
        return (found & (tile >= 0)).astype(jnp.int32)

    start = jnp.int32(0)
    clip_start = jnp.int32(0)
    clip_text = jnp.int32(0)
    for c in range(clip_ref.shape[0]):
        length = clip_ref[c]
        inside = ((start <= me) & (me < start + length)).astype(jnp.int32)
        clip_start = clip_start + inside * start
        clip_text = clip_text + inside * text_ref[c]
        start = start + length
    text_low = clip_start * trows
    text_high = text_low + clip_text

    def bias_of(flag):
        return (1.0 - flag.astype(jnp.float32)) * LOW

    bias_own = jnp.zeros((1, rows), jnp.float32)
    bias_near = [jnp.full((1, rows), bias_of(listed(me - by)), jnp.float32) for by in (1, -1)]
    bias_far = [
        jnp.full(
            (1, rows), bias_of(jnp.maximum(listed(me - by), listed(me - by - by // 2))), jnp.float32
        )
        for by in (2, -2)
    ]
    place = lax.broadcasted_iota(jnp.int32, (1, text_pad), 1)
    row = (me - (MOST - 1)) * trows + place
    owned = (row >= text_low) & (row < text_high) & (place < SPAN * trows)
    bias_text = jnp.where(owned, 0.0, LOW)
    bias_one = jnp.concatenate([bias_own] + bias_near, axis=1)
    bias_two = jnp.concatenate(bias_far, axis=1)
    own_share = [jnp.full((16, cw), listed(me + by).astype(jnp.float32)) for by in (2, -2)]

    scale = HD ** (-0.5) * 1.4426950408889634
    block = 128 if rows % 128 == 0 else rows
    blocks = rows // block

    def score(q_part, k_part, bias):
        s = lax.dot_general(
            q_part, k_part, (((1,), (1,)), ((), ())), preferred_element_type=jnp.float32
        )
        return s * scale + bias

    def weigh(p, v_part):
        return jnp.dot(p.astype(jnp.bfloat16), v_part, preferred_element_type=jnp.float32)

    def first(c):
        def one(i, carry):
            h = c * group + i // blocks
            at = pl.ds(pl.multiple_of(h * HD, HD), HD)
            qr = pl.ds(pl.multiple_of(lax.rem(i, blocks) * block, block), block)
            s = score(q[qr, at], kv[0, pl.ds(0, 3 * rows), at], bias_one)
            m = jnp.max(s, axis=1, keepdims=True)
            p = jnp.exp2(s - m)
            top[qr, at] = jnp.broadcast_to(m, (block, HD))
            total[qr, at] = jnp.broadcast_to(jnp.sum(p, axis=1, keepdims=True), (block, HD))
            acc[qr, at] = weigh(p, kv[1, pl.ds(0, 3 * rows), at])
            return carry

        lax.fori_loop(0, group * blocks, one, 0)

    def second(c):
        def one(i, carry):
            h = c * group + i // blocks
            at = pl.ds(pl.multiple_of(h * HD, HD), HD)
            qr = pl.ds(pl.multiple_of(lax.rem(i, blocks) * block, block), block)
            q_part = q[qr, at]
            far = pl.ds(3 * rows, 2 * rows)
            s1 = score(q_part, kv[0, far, at], bias_two)
            s2 = score(q_part, text[0, :, at], bias_text)
            before = top[qr, at]
            m = jnp.maximum(
                jnp.maximum(jnp.max(s1, axis=1, keepdims=True), jnp.max(s2, axis=1, keepdims=True)),
                before,
            )
            fade = jnp.exp2(before - m)
            p1 = jnp.exp2(s1 - m[:, :1])
            p2 = jnp.exp2(s2 - m[:, :1])
            l = (
                total[qr, at] * fade
                + jnp.sum(p1, axis=1, keepdims=True)
                + jnp.sum(p2, axis=1, keepdims=True)
            )
            a = acc[qr, at] * fade + weigh(p1, kv[1, far, at]) + weigh(p2, text[1, :, at])
            attended[qr, at] = (a / l).astype(jnp.bfloat16)
            return carry

        lax.fori_loop(0, group * blocks, one, 0)

    for copy in own_copies[:3]:
        copy.wait()

    step = 1
    for c in range(chunks):
        for by in (1, -1):

            @pl.when(exists(-by))
            def _():
                for j in range(2):
                    near_copy(by, c, j).wait_recv()

        cols = pl.ds(c * cw, cw)
        for i, by in enumerate((1, -1)):

            @pl.when(exists(2 * by))
            def _():
                def mix(r, carry):
                    mine = own_share[i].astype(jnp.bfloat16)
                    for j in range(2):
                        a = kv[j, pl.ds(pl.multiple_of(r * 16, 16), 16), cols]
                        b = kv[
                            j, pl.ds(pl.multiple_of(near_slot(by) * rows + r * 16, 16), 16), cols
                        ]
                        stage[i, j, pl.ds(pl.multiple_of(r * 16, 16), 16), cols] = (
                            a * mine + b * (1 - mine)
                        )
                    return carry

                lax.fori_loop(0, rows // 16, mix, 0)
                for j in range(2):
                    far_copy(2 * by, c, j).start()

        for _ in range(2 if c == 0 else 1):
            if step < MOST - 1:
                text_arrive(step)
                step += 1
                text_start(step)
        first(c)
    while step < MOST - 1:
        text_arrive(step)
        step += 1
        text_start(step)
    text_arrive(MOST - 1)

    for c in range(chunks):
        for by in (2, -2):

            @pl.when(exists(-by))
            def _():
                for j in range(2):
                    far_copy(by, c, j).wait_recv()

        second(c)

    w_copy.wait()
    wide = w.shape[1]
    parts = 4
    pw = wide // parts
    out_rows = rows // n_head

    def out_copy(d, p):
        peer = lax.rem(head + d, n_head)
        return pltpu.make_async_remote_copy(
            src_ref=partial.at[peer, :, pl.ds(p * pw, pw)],
            dst_ref=arrived.at[d - 1, :, pl.ds(p * pw, pw)],
            send_sem=out_send.at[d - 1, p],
            recv_sem=out_recv.at[d - 1, p],
            device_id={"head": peer},
            device_id_type=MESH,
        )

    for p in range(parts):
        for g in range(n_head):
            partial[g, :, pl.ds(p * pw, pw)] = jnp.dot(
                attended[pl.ds(g * out_rows, out_rows), :],
                w[:, pl.ds(p * pw, pw)],
                preferred_element_type=jnp.float32,
            ).astype(jnp.bfloat16)
        for d in range(1, n_head):
            out_copy(d, p).start()
    for p in range(parts):
        sums = partial[head, :, pl.ds(p * pw, pw)].astype(jnp.float32)
        for d in range(1, n_head):
            out_copy(d, p).wait_recv()
            sums = sums + arrived[d - 1, :, pl.ds(p * pw, pw)].astype(jnp.float32)
        out_ref[:, pl.ds(p * pw, pw)] = sums.astype(jnp.bfloat16)

    for by in (1, -1):

        @pl.when(exists(by))
        def _():
            for c in range(chunks):
                for j in range(2):
                    near_copy(by, c, j).wait_send()

        @pl.when(exists(2 * by))
        def _():
            for c in range(chunks):
                for j in range(2):
                    far_copy(2 * by, c, j).wait_send()

        for s in range(1, MOST):

            @pl.when(exists(by) & exists(-by * (s - 1)))
            def _():
                for j in range(2):
                    text_copy(by, s, j).wait_send()

    for p in range(parts):
        for d in range(1, n_head):
            out_copy(d, p).wait_send()


def body(n_seq, n_head, q, k, v, tk, tv, near, clip_lengths, text_lengths, w):
    rows, width = q.shape
    heads = width // HD
    group = GROUP if heads % GROUP == 0 else 1
    chunks = heads // group
    wide = w.shape[1]
    out_rows = rows // n_head
    text_pad = -(-SPAN * tk.shape[0] // 128) * 128
    smem = pl.BlockSpec(memory_space=pltpu.SMEM)
    hbm = pl.BlockSpec(memory_space=pl.ANY)
    dma = pltpu.SemaphoreType.DMA
    bf16, f32 = jnp.bfloat16, jnp.float32
    return pl.pallas_call(
        functools.partial(kernel, n_seq, n_head),
        out_shape=jax.ShapeDtypeStruct((out_rows, wide), bf16),
        in_specs=[smem] * 3 + [hbm] * 6,
        out_specs=pl.BlockSpec(memory_space=pltpu.VMEM),
        scratch_shapes=[
            pltpu.VMEM((rows, width), bf16),
            pltpu.VMEM((2, 5 * rows, width), bf16),
            pltpu.VMEM((2, text_pad, width), bf16),
            pltpu.VMEM((2, 2, rows, width), bf16),
            pltpu.VMEM(w.shape, bf16),
            pltpu.VMEM((rows, width), f32),
            pltpu.VMEM((rows, width), f32),
            pltpu.VMEM((rows, width), f32),
            pltpu.VMEM((rows, width), bf16),
            pltpu.VMEM((n_head, out_rows, wide), bf16),
            pltpu.VMEM((n_head - 1, out_rows, wide), bf16),
            dma((2, chunks, 2)),
            dma((2, chunks, 2)),
            dma((2, chunks, 2)),
            dma((2, chunks, 2)),
            dma((2, MOST - 1, 2)),
            dma((2, MOST - 1, 2)),
            dma((n_head - 1, 4)),
            dma((n_head - 1, 4)),
            dma((6,)),
        ],
        compiler_params=pltpu.CompilerParams(
            collective_id=0, has_side_effects=True, vmem_limit_bytes=58 << 20
        ),
    )(near, clip_lengths, text_lengths, q, k, v, tk, tv, w)


def solution(mesh):
    placed = (
        P("seq", "head"),
        P("seq", "head"),
        P("seq", "head"),
        P("seq", "head"),
        P("seq", "head"),
        P("seq", None),
        P(),
        P(),
        P("head", None),
    )
    return jax.shard_map(
        functools.partial(body, mesh.shape["seq"], mesh.shape["head"]),
        mesh=mesh,
        in_specs=placed,
        out_specs=P(("seq", "head"), None),
        check_vma=False,
    )
```

time: 511 us -> 243 us (0.48)
  the two profiles are of different devices: /device:TPU:0 before, /device:TPU:15 now
where the time goes in v1:
time: 243 us; the launch traced here: 239 us
  Pallas kernels  236 us (97%)
    pallas_call x1, Pallas kernels, body(): pl.pallas_call(functools.partial(kernel, n_seq, n_head), out_shape=jax.Sh...  236 us

profile of v1, /device:TPU:15, one launch (start us, length us, event | category | flops | bytes accessed | tf_op | source)
XLA Modules:
  0.0 238.9 jit_solution(3629207051958263199)
XLA Ops:
  0.0 236.5 %shard_map.91 = bf16[192,3072]{1,0:T(8,128)(2,1)} custom-call(s32[1,5]{1,0:T(1,128)} %near_ref.1, s32[4]{0:T(128)} %clip_ref.1, s32[4]{0:T(128)} %text_ref.1, bf16[384,1536]{1,0:T(8,128)(2,1)} %q_hbm.1, bf16[384,1536]{1,0:T(8,128)(2,1)} %k_hbm.1, bf16[384,1536]{1,0:T(8,128)(2,1)} %v_hbm.1, bf16[32,1536]{1,0:T(8,128)(2,1)} %tk_hbm.1, ...), custom_call_target="tpu_custom_call" | custom-call | tf_op jit(solution)/shard_map/pallas_call | solution.py:386
  236.5 2.4 copy.11

commit v2 on v1

v2 whole, which is shorter than its diff:
```python
import functools

import jax
import jax.numpy as jnp
from jax import lax
from jax.experimental import pallas as pl
from jax.experimental.pallas import tpu as pltpu
from jax.sharding import PartitionSpec as P

HD = 128
MOST = 7
PLANE = 4
PLANES_AROUND = 2
COLUMN = 2 * PLANES_AROUND + 1
GROUP = 2
LOW = -1e30
MESH = pl.DeviceIdType.MESH


def kernel(
    n_seq,
    n_head,
    near_ref,
    clip_ref,
    text_ref,
    q_hbm,
    k_hbm,
    v_hbm,
    tk_hbm,
    tv_hbm,
    w_hbm,
    list_hbm,
    out_ref,
    q,
    kv,
    text,
    stage,
    w,
    acc,
    top,
    total,
    attended,
    partial,
    arrived,
    passed,
    peer_list,
    near_send,
    near_recv,
    edge_send,
    edge_recv,
    far_send,
    far_recv,
    text_send,
    text_recv,
    pass_send,
    pass_recv,
    list_sem,
    out_send,
    out_recv,
    local_sem,
):
    me = lax.axis_index("seq")
    head = lax.axis_index("head")
    rows, width = q.shape
    heads = width // HD
    group = GROUP if heads % GROUP == 0 else 1
    chunks = heads // group
    cw = group * HD
    trows = tk_hbm.shape[0]
    text_pad = text.shape[1]
    j4 = lax.rem(me, PLANE)
    base = me - j4
    low_half = j4 < PLANE // 2

    def exists(by):
        return (me + by >= 0) & (me + by < n_seq)

    def side(i):
        return low_half if i == 0 else jnp.logical_not(low_half)

    def at_place(by, place):
        return j4 == (place if by == 1 else PLANE - 1 - place)

    def near_slot(by):
        return 1 if by == 1 else 2

    def far_slot(by):
        return 3 if by == 1 else 4

    mid = PLANES_AROUND * trows
    own_copies = [
        pltpu.make_async_copy(q_hbm, q, local_sem.at[0]),
        pltpu.make_async_copy(k_hbm, kv.at[0, pl.ds(0, rows)], local_sem.at[1]),
        pltpu.make_async_copy(v_hbm, kv.at[1, pl.ds(0, rows)], local_sem.at[2]),
        pltpu.make_async_copy(tk_hbm, text.at[0, pl.ds(mid, trows)], local_sem.at[3]),
        pltpu.make_async_copy(tv_hbm, text.at[1, pl.ds(mid, trows)], local_sem.at[4]),
    ]
    w_copy = pltpu.make_async_copy(w_hbm, w, local_sem.at[5])
    text[...] = jnp.zeros_like(text)
    for copy in own_copies:
        copy.start()

    def blank(slot):
        kv[:, pl.ds(slot * rows, rows), :] = jnp.zeros((2, rows, width), kv.dtype)

    for by in (1, -1):

        @pl.when(jnp.logical_not(exists(-by)))
        def _():
            blank(near_slot(by))

        @pl.when(side(0 if by == 1 else 1) & jnp.logical_not(exists(-PLANE * by)))
        def _():
            blank(far_slot(by))

    peer_list[...] = jnp.full(peer_list.shape, -1, jnp.int32)

    barrier = pltpu.get_barrier_semaphore()
    partners = n_head - 1
    for step in (1, 2, 3, 4):
        for by in (step, -step):
            partners = partners + exists(by).astype(jnp.int32)

            @pl.when(exists(by))
            def _():
                pl.semaphore_signal(barrier, inc=1, device_id={"seq": me + by}, device_id_type=MESH)

    for d in range(1, n_head):
        pl.semaphore_signal(
            barrier, inc=1, device_id={"head": lax.rem(head + d, n_head)}, device_id_type=MESH
        )
    pl.semaphore_wait(barrier, partners)

    def push(src, dst, sem, at, to):
        return pltpu.make_async_remote_copy(
            src_ref=src,
            dst_ref=dst,
            send_sem=sem[0].at[at],
            recv_sem=sem[1].at[at],
            device_id={"seq": to},
            device_id_type=MESH,
        )

    near_sem = (near_send, near_recv)
    edge_sem = (edge_send, edge_recv)
    far_sem = (far_send, far_recv)
    text_sem = (text_send, text_recv)
    pass_sem = (pass_send, pass_recv)

    def slot_at(n, c, j):
        return kv.at[j, pl.ds(n * rows, rows), pl.ds(c * cw, cw)]

    def near_copy(by, c, j):
        src = (k_hbm if j == 0 else v_hbm).at[:, pl.ds(c * cw, cw)]
        i = 0 if by == 1 else 1
        return push(src, slot_at(near_slot(by), c, j), near_sem, (i, c, j), me + by)

    def edge_copy(by, c, j):
        i = 0 if by == 1 else 1
        src = slot_at(near_slot(-by), c, j)
        return push(src, slot_at(near_slot(by), c, j), edge_sem, (i, c, j), me + 2 * by)

    def far_copy(by, c, j):
        src = stage.at[0, j, :, pl.ds(c * cw, cw)]
        return push(src, slot_at(far_slot(by), c, j), far_sem, (0, c, j), me + 2 * by)

    def over_copy(by, c, j):
        src = stage.at[1, j, :, pl.ds(c * cw, cw)]
        return push(src, slot_at(far_slot(by), c, j), far_sem, (1, c, j), me + PLANE * by)

    def list_copy(by):
        return pltpu.make_async_remote_copy(
            src_ref=list_hbm,
            dst_ref=peer_list,
            send_sem=list_sem.at[0],
            recv_sem=list_sem.at[1],
            device_id={"seq": me - PLANE * by},
            device_id_type=MESH,
        )

    def column_copy(by, step, j):
        i = 0 if by == 1 else 1
        at = PLANES_AROUND - by * (step - 1)
        return push(
            text.at[j, pl.ds(at * trows, trows)],
            text.at[j, pl.ds((at - by) * trows, trows)],
            text_sem,
            (i, step - 1, j),
            me + PLANE * by,
        )

    def pass_copy(m, j):
        return push(
            passed.at[j, pl.ds((m - 1) * 2 * trows, 2 * trows)],
            text.at[j, pl.ds((COLUMN + 2 * (m - 1)) * trows, 2 * trows)],
            pass_sem,
            (m - 1, j),
            base + lax.rem(j4 + m, PLANE),
        )

    def column_start(step):
        for by in (1, -1):

            @pl.when(exists(PLANE * by) & exists(-PLANE * by * (step - 1)))
            def _():
                for j in range(2):
                    column_copy(by, step, j).start()

    def column_arrive(step):
        for by in (1, -1):

            @pl.when(exists(-PLANE * by * step))
            def _():
                for j in range(2):
                    column_copy(by, step, j).wait_recv()

    for copy in own_copies[3:]:
        copy.wait()
    for i, by in enumerate((1, -1)):

        @pl.when(side(i) & exists(-PLANE * by))
        def _():
            list_copy(by).start()

    column_start(1)
    for c in range(chunks):
        for by in (1, -1):

            @pl.when(jnp.logical_not(at_place(by, PLANE - 1)))
            def _():
                for j in range(2):
                    near_copy(by, c, j).start()

    w_copy.start()

    def listed(tile):
        found = near_ref[0, 0] == tile
        for i in range(1, near_ref.shape[1]):
            found = found | (near_ref[0, i] == tile)
        return (found & (tile >= 0)).astype(jnp.int32)

    def clip_of(tile):
        start = jnp.int32(0)
        first_tile = jnp.int32(0)
        count = jnp.int32(0)
        for c in range(clip_ref.shape[0]):
            length = clip_ref[c]
            inside = ((start <= tile) & (tile < start + length)).astype(jnp.int32)
            first_tile = first_tile + inside * start
            count = count + inside * text_ref[c]
            start = start + length
        return first_tile, count

    def in_column(first_tile, column):
        return first_tile + lax.rem(column + PLANE * n_seq - first_tile, PLANE)

    clip_start, clip_text = clip_of(me)
    text_low = clip_start * trows
    text_high = text_low + clip_text

    def bias_of(flag):
        return (1.0 - flag.astype(jnp.float32)) * LOW

    bias_own = jnp.zeros((1, rows), jnp.float32)
    bias_near = [jnp.full((1, rows), bias_of(listed(me - by)), jnp.float32) for by in (1, -1)]
    bias_far = [
        jnp.full(
            (1, rows), bias_of(jnp.maximum(listed(me - by), listed(me - by - by // 2))), jnp.float32
        )
        for by in (2, -2)
    ]
    place = lax.broadcasted_iota(jnp.int32, (1, text_pad), 1)
    shift = jnp.full((1, text_pad), -1, jnp.int32)
    tiles = [me + PLANE * (d - PLANES_AROUND) for d in range(COLUMN)]
    for m in range(1, PLANE):
        origin = in_column(clip_start, lax.rem(j4 + PLANE - m, PLANE))
        tiles += [origin, origin + PLANE]
    for n, tile in enumerate(tiles):
        here = (place >= n * trows) & (place < (n + 1) * trows)
        shift = jnp.where(here, (tile - n) * trows + place, shift)
    bias_text = jnp.where((shift >= text_low) & (shift < text_high), 0.0, LOW)
    bias_one = jnp.concatenate([bias_own] + bias_near, axis=1)
    bias_two = jnp.concatenate(bias_far, axis=1)
    own_share = jnp.full(
        (16, cw), jnp.maximum(listed(me + 2), listed(me - 2)).astype(jnp.float32)
    ).astype(jnp.bfloat16)

    scale = HD ** (-0.5) * 1.4426950408889634
    block = 128 if rows % 128 == 0 else rows
    blocks = rows // block

    def score(q_part, k_part, bias):
        s = lax.dot_general(
            q_part, k_part, (((1,), (1,)), ((), ())), preferred_element_type=jnp.float32
        )
        return s * scale + bias

    def weigh(p, v_part):
        return jnp.dot(p.astype(jnp.bfloat16), v_part, preferred_element_type=jnp.float32)

    def first(c):
        def one(i, carry):
            h = c * group + i // blocks
            at = pl.ds(pl.multiple_of(h * HD, HD), HD)
            qr = pl.ds(pl.multiple_of(lax.rem(i, blocks) * block, block), block)
            s = score(q[qr, at], kv[0, pl.ds(0, 3 * rows), at], bias_one)
            m = jnp.max(s, axis=1, keepdims=True)
            p = jnp.exp2(s - m)
            top[qr, at] = jnp.broadcast_to(m, (block, HD))
            total[qr, at] = jnp.broadcast_to(jnp.sum(p, axis=1, keepdims=True), (block, HD))
            acc[qr, at] = weigh(p, kv[1, pl.ds(0, 3 * rows), at])
            return carry

        lax.fori_loop(0, group * blocks, one, 0)

    def second(c):
        def one(i, carry):
            h = c * group + i // blocks
            at = pl.ds(pl.multiple_of(h * HD, HD), HD)
            qr = pl.ds(pl.multiple_of(lax.rem(i, blocks) * block, block), block)
            q_part = q[qr, at]
            far = pl.ds(3 * rows, 2 * rows)
            s1 = score(q_part, kv[0, far, at], bias_two)
            s2 = score(q_part, text[0, :, at], bias_text)
            before = top[qr, at]
            m = jnp.maximum(
                jnp.maximum(jnp.max(s1, axis=1, keepdims=True), jnp.max(s2, axis=1, keepdims=True)),
                before,
            )
            fade = jnp.exp2(before - m)
            p1 = jnp.exp2(s1 - m[:, :1])
            p2 = jnp.exp2(s2 - m[:, :1])
            l = (
                total[qr, at] * fade
                + jnp.sum(p1, axis=1, keepdims=True)
                + jnp.sum(p2, axis=1, keepdims=True)
            )
            a = acc[qr, at] * fade + weigh(p1, kv[1, far, at]) + weigh(p2, text[1, :, at])
            attended[qr, at] = (a / l).astype(jnp.bfloat16)
            return carry

        lax.fori_loop(0, group * blocks, one, 0)

    def pass_text():
        for m in range(1, PLANE):
            first_tile, _ = clip_of(base + lax.rem(j4 + m, PLANE))
            plane = lax.div(in_column(first_tile, j4) + PLANE * n_seq - me, PLANE) - n_seq
            for extra in range(2):
                for j in range(2):
                    picked = jnp.zeros((trows, width), jnp.bfloat16)
                    for d in range(COLUMN):
                        share = (plane + extra == d - PLANES_AROUND).astype(jnp.float32)
                        share = jnp.full((trows, width), share).astype(jnp.bfloat16)
                        picked = picked + share * text[j, pl.ds(d * trows, trows), :]
                    passed[j, pl.ds((2 * (m - 1) + extra) * trows, trows), :] = picked
            for j in range(2):
                pass_copy(m, j).start()

    def mix(share, n, slot_one, slot_two, c):
        cols = pl.ds(c * cw, cw)

        def one(r, carry):
            for j in range(2):
                a = kv[j, pl.ds(pl.multiple_of(slot_one * rows + r * 16, 16), 16), cols]
                b = kv[j, pl.ds(pl.multiple_of(slot_two * rows + r * 16, 16), 16), cols]
                stage[n, j, pl.ds(pl.multiple_of(r * 16, 16), 16), cols] = a * share + b * (
                    1 - share
                )
            return carry

        lax.fori_loop(0, rows // 16, one, 0)

    def near_stage(c):
        for by in (1, -1):

            @pl.when(jnp.logical_not(at_place(by, 0)))
            def _():
                for j in range(2):
                    near_copy(by, c, j).wait_recv()

        for by in (1, -1):

            @pl.when(at_place(by, PLANE - 2) & exists(2 * by))
            def _():
                for j in range(2):
                    edge_copy(by, c, j).start()

    def far_stage(c):
        for i, by in enumerate((1, -1)):

            @pl.when(at_place(by, 0) & exists(-by))
            def _():
                for j in range(2):
                    edge_copy(by, c, j).wait_recv()

        for i, by in enumerate((1, -1)):

            @pl.when(side(i))
            def _():
                mix(own_share, 0, 0, near_slot(by), c)
                for j in range(2):
                    far_copy(by, c, j).start()

    def over_stage(c):
        for i, by in enumerate((1, -1)):

            @pl.when(side(i))
            def _():
                for j in range(2):
                    far_copy(-by, c, j).wait_recv()

            @pl.when(side(i) & exists(PLANE * by))
            def _():
                wanted = (peer_list[...] == me + 2 * by).astype(jnp.float32)
                wanted = jnp.max(jnp.max(wanted, axis=1, keepdims=True), axis=0, keepdims=True)
                share = jnp.broadcast_to(wanted, (16, cw)).astype(jnp.bfloat16)
                mix(share, 1, far_slot(-by), near_slot(-by), c)
                for j in range(2):
                    over_copy(by, c, j).start()

    def last_stage(c):
        for i, by in enumerate((1, -1)):

            @pl.when(side(i) & exists(-PLANE * by))
            def _():
                for j in range(2):
                    over_copy(by, c, j).wait_recv()

    column_arrive(1)
    column_start(2)
    for copy in own_copies[:3]:
        copy.wait()
    for i, by in enumerate((1, -1)):

        @pl.when(side(i) & exists(PLANE * by))
        def _():
            list_copy(by).wait_recv()

    for turn in range(chunks + 3):
        if turn < chunks:
            near_stage(turn)
        if 0 <= turn - 1 < chunks:
            far_stage(turn - 1)
        if turn == 1:
            column_arrive(2)
            pass_text()
        if 0 <= turn - 2 < chunks:
            over_stage(turn - 2)
        if 0 <= turn - 1 < chunks:
            first(turn - 1)
        if turn == 3:
            for m in range(1, PLANE):
                for j in range(2):
                    pass_copy(m, j).wait_recv()
        if 0 <= turn - 3:
            last_stage(turn - 3)
            second(turn - 3)

    w_copy.wait()
    wide = w.shape[1]
    parts = 4
    pw = wide // parts
    out_rows = rows // n_head

    def out_copy(d, p):
        peer = lax.rem(head + d, n_head)
        return pltpu.make_async_remote_copy(
            src_ref=partial.at[peer, :, pl.ds(p * pw, pw)],
            dst_ref=arrived.at[d - 1, :, pl.ds(p * pw, pw)],
            send_sem=out_send.at[d - 1, p],
            recv_sem=out_recv.at[d - 1, p],
            device_id={"head": peer},
            device_id_type=MESH,
        )

    for p in range(parts):
        for g in range(n_head):
            partial[g, :, pl.ds(p * pw, pw)] = jnp.dot(
                attended[pl.ds(g * out_rows, out_rows), :],
                w[:, pl.ds(p * pw, pw)],
                preferred_element_type=jnp.float32,
            ).astype(jnp.bfloat16)
        for d in range(1, n_head):
            out_copy(d, p).start()
    for p in range(parts):
        sums = partial[head, :, pl.ds(p * pw, pw)].astype(jnp.float32)
        for d in range(1, n_head):
            out_copy(d, p).wait_recv()
            sums = sums + arrived[d - 1, :, pl.ds(p * pw, pw)].astype(jnp.float32)
        out_ref[:, pl.ds(p * pw, pw)] = sums.astype(jnp.bfloat16)

    for i, by in enumerate((1, -1)):

        @pl.when(side(i) & exists(-PLANE * by))
        def _():
            list_copy(by).wait_send()

        @pl.when(jnp.logical_not(at_place(by, PLANE - 1)))
        def _():
            for c in range(chunks):
                for j in range(2):
                    near_copy(by, c, j).wait_send()

        @pl.when(at_place(by, PLANE - 2) & exists(2 * by))
        def _():
            for c in range(chunks):
                for j in range(2):
                    edge_copy(by, c, j).wait_send()

        @pl.when(side(i))
        def _():
            for c in range(chunks):
                for j in range(2):
                    far_copy(by, c, j).wait_send()

        @pl.when(side(i) & exists(PLANE * by))
        def _():
            for c in range(chunks):
                for j in range(2):
                    over_copy(by, c, j).wait_send()

        for step in range(1, PLANES_AROUND + 1):

            @pl.when(exists(PLANE * by) & exists(-PLANE * by * (step - 1)))
            def _():
                for j in range(2):
                    column_copy(by, step, j).wait_send()

    for m in range(1, PLANE):
        for j in range(2):
            pass_copy(m, j).wait_send()

    for p in range(parts):
        for d in range(1, n_head):
            out_copy(d, p).wait_send()


def body(n_seq, n_head, q, k, v, tk, tv, near, clip_lengths, text_lengths, w):
    rows, width = q.shape
    heads = width // HD
    group = GROUP if heads % GROUP == 0 else 1
    chunks = heads // group
    wide = w.shape[1]
    out_rows = rows // n_head
    trows = tk.shape[0]
    text_pad = -(-(COLUMN + 2 * (PLANE - 1)) * trows // 128) * 128
    padded = jnp.pad(near, ((0, 7), (0, 128 - near.shape[1])), constant_values=-1)
    smem = pl.BlockSpec(memory_space=pltpu.SMEM)
    hbm = pl.BlockSpec(memory_space=pl.ANY)
    dma = pltpu.SemaphoreType.DMA
    bf16, f32 = jnp.bfloat16, jnp.float32
    return pl.pallas_call(
        functools.partial(kernel, n_seq, n_head),
        out_shape=jax.ShapeDtypeStruct((out_rows, wide), bf16),
        in_specs=[smem] * 3 + [hbm] * 7,
        out_specs=pl.BlockSpec(memory_space=pltpu.VMEM),
        scratch_shapes=[
            pltpu.VMEM((rows, width), bf16),
            pltpu.VMEM((2, 5 * rows, width), bf16),
            pltpu.VMEM((2, text_pad, width), bf16),
            pltpu.VMEM((2, 2, rows, width), bf16),
            pltpu.VMEM(w.shape, bf16),
            pltpu.VMEM((rows, width), f32),
            pltpu.VMEM((rows, width), f32),
            pltpu.VMEM((rows, width), f32),
            pltpu.VMEM((rows, width), bf16),
            pltpu.VMEM((n_head, out_rows, wide), bf16),
            pltpu.VMEM((n_head - 1, out_rows, wide), bf16),
            pltpu.VMEM((2, 2 * (PLANE - 1) * trows, width), bf16),
            pltpu.VMEM((8, 128), jnp.int32),
            dma((2, chunks, 2)),
            dma((2, chunks, 2)),
            dma((2, chunks, 2)),
            dma((2, chunks, 2)),
            dma((2, chunks, 2)),
            dma((2, chunks, 2)),
            dma((2, PLANES_AROUND, 2)),
            dma((2, PLANES_AROUND, 2)),
            dma((PLANE - 1, 2)),
            dma((PLANE - 1, 2)),
            dma((2,)),
            dma((n_head - 1, 4)),
            dma((n_head - 1, 4)),
            dma((6,)),
        ],
        compiler_params=pltpu.CompilerParams(
            collective_id=0, has_side_effects=True, vmem_limit_bytes=58 << 20
        ),
    )(near, clip_lengths, text_lengths, q, k, v, tk, tv, w, padded)


def solution(mesh):
    placed = (
        P("seq", "head"),
        P("seq", "head"),
        P("seq", "head"),
        P("seq", "head"),
        P("seq", "head"),
        P("seq", None),
        P(),
        P(),
        P("head", None),
    )
    return jax.shard_map(
        functools.partial(body, mesh.shape["seq"], mesh.shape["head"]),
        mesh=mesh,
        in_specs=placed,
        out_specs=P(("seq", "head"), None),
        check_vma=False,
    )
```

time: 243 us -> 198 us (0.81); the launches traced: 239 us -> 197 us
  Pallas kernels: 236 us -> 194 us
    pallas_call x1, Pallas kernels: 236 us -> 194 us  [body(): pl.pallas_call(functools.partial(kernel, n_seq, n_head), out_shape=jax.Sh...]
where the time goes in v2:
time: 198 us; the launch traced here: 197 us
  Pallas kernels  194 us (98%)
  local copies, waits for them, and re-layouts  3.61 us (2%)
    pallas_call x1, Pallas kernels, body(): pl.pallas_call(functools.partial(kernel, n_seq, n_head), out_shape=jax.Sh...  194 us

profile of v2, /device:TPU:15, one launch (start us, length us, event | category | flops | bytes accessed | tf_op | source)
XLA Modules:
  0.0 197.5 jit_solution(8292505967999063141)
XLA Ops:
  0.0 1.3 pad.4.list_hbm
  1.3 193.8 %shard_map.91 = bf16[192,3072]{1,0:T(8,128)(2,1)} custom-call(s32[1,5]{1,0:T(1,128)} %near_ref.1, s32[4]{0:T(128)} %clip_ref.1, s32[4]{0:T(128)} %text_ref.1, bf16[384,1536]{1,0:T(8,128)(2,1)} %q_hbm.1, bf16[384,1536]{1,0:T(8,128)(2,1)} %k_hbm.1, bf16[384,1536]{1,0:T(8,128)(2,1)} %v_hbm.1, bf16[32,1536]{1,0:T(8,128)(2,1)} %tk_hbm.1, ...), custom_call_target="tpu_custom_call" | custom-call | tf_op jit(solution)/shard_map/pallas_call | solution.py:552
  195.1 2.4 %copy.11 = bf16[192,3072]{1,0:T(8,128)(2,1)} copy(bf16[192,3072]{1,0:T(8,128)(2,1)} %shard_map.91) | data formatting | bytes 2359296

commit v3 on v2

--- a/solution.py
+++ b/solution.py
@@ -13,6 +13,7 @@
 PLANES_AROUND = 2
 COLUMN = 2 * PLANES_AROUND + 1
 GROUP = 2
+AHEAD = 2
 LOW = -1e30
 MESH = pl.DeviceIdType.MESH
 
@@ -223,7 +224,7 @@
             list_copy(by).start()
 
     column_start(1)
-    for c in range(chunks):
+    def near_start(c):
         for by in (1, -1):
 
             @pl.when(jnp.logical_not(at_place(by, PLANE - 1)))
@@ -231,6 +232,8 @@
                 for j in range(2):
                     near_copy(by, c, j).start()
 
+    for c in range(min(AHEAD, chunks)):
+        near_start(c)
     w_copy.start()
 
     def listed(tile):
@@ -446,6 +449,8 @@
             pass_text()
         if 0 <= turn - 2 < chunks:
             over_stage(turn - 2)
+        if turn + AHEAD < chunks:
+            near_start(turn + AHEAD)
         if 0 <= turn - 1 < chunks:
             first(turn - 1)
         if turn == 3:

time: 198 us -> 177 us (0.89)
  Pallas kernels: 194 us -> 173 us
    pallas_call x1, Pallas kernels: 194 us -> 173 us  [body(): pl.pallas_call(functools.partial(kernel, n_seq, n_head), out_shape=jax.Sh...]
where the time goes in v3:
time: 177 us; the launch traced here: 176 us
  Pallas kernels  173 us (98%)
  local copies, waits for them, and re-layouts  3.61 us (2%)
    pallas_call x1, Pallas kernels, body(): pl.pallas_call(functools.partial(kernel, n_seq, n_head), out_shape=jax.Sh...  173 us

profile of v3, /device:TPU:15, one launch (start us, length us, event | category | flops | bytes accessed | tf_op | source)
XLA Modules:
  0.0 176.5 jit_solution(16229403602630276877)
XLA Ops:
  0.0 1.3 pad.4.list_hbm
  1.3 172.8 %shard_map.91 = bf16[192,3072]{1,0:T(8,128)(2,1)} custom-call(s32[1,5]{1,0:T(1,128)} %near_ref.1, s32[4]{0:T(128)} %clip_ref.1, s32[4]{0:T(128)} %text_ref.1, bf16[384,1536]{1,0:T(8,128)(2,1)} %q_hbm.1, bf16[384,1536]{1,0:T(8,128)(2,1)} %k_hbm.1, bf16[384,1536]{1,0:T(8,128)(2,1)} %v_hbm.1, bf16[32,1536]{1,0:T(8,128)(2,1)} %tk_hbm.1, ...), custom_call_target="tpu_custom_call" | custom-call | tf_op jit(solution)/shard_map/pallas_call | solution.py:557
  174.1 2.4 %copy.11 = bf16[192,3072]{1,0:T(8,128)(2,1)} copy(bf16[192,3072]{1,0:T(8,128)(2,1)} %shard_map.91) | data formatting | bytes 2359296
